TPU v7x, 32 devices: a whole 2x2x4 slice. The times are simulated.
32 devices in a mesh: kset: 2 (over y), grid: 16 (over z, x, core).
Axes of the slice: x: 2, y: 2, z: 4, core: 2. Of those that a mesh axis runs over, the one named last changes fastest.
Arguments:
- bands: bfloat16 [4, 4096, 1536], P('kset', 'grid'), parts along dimension 0, may hold values from -4 to 4, as said below
- hbands: bfloat16 [4, 4096, 1536], P('kset', 'grid'), parts along dimension 0, may hold values from -10 to 10, as said below
- occupied: int32 [4], P('kset'), parts along dimension 0, may hold values from 192 to 576
Outputs:
- new_bands: bfloat16 [4, 4096, 1536], P('kset', 'grid'), parts along dimension 0
There are 2 independent parts, one for each index of `kset`. A program takes and returns all parts, laid end to end along the dimension named above; each array names one. Nothing has to cross between parts.
Inputs may be any that keep to these rules, and one draw needn't show every extreme that they name: `bands`: real values on every grid point. `hbands`: real values on every grid point.
All inputs are finite; a program needn't handle non-finite values.
Results may differ from a plain program's by a relative error of at most 0.0079.
Values may be sent and summed in bfloat16 or wider, within the bound.
A program may use at most 64 MiB of HBM per device.

v0:
```python
import jax
import jax.numpy as jnp
from jax import lax
from jax.sharding import PartitionSpec as P

MCW = 2


def embedding(full):
    width = full.shape[-1] // 2
    real_part = full[..., :width]
    imag_part = full[..., width:]
    upper = jnp.concatenate([real_part, imag_part], -1)
    lower = jnp.concatenate([-imag_part, real_part], -1)
    return jnp.concatenate([upper, lower], -2)


def on_device(bands, hbands, occupied):
    points, local_rows, columns = bands.shape
    half = columns // 2
    devices = lax.axis_size("grid")
    share = half // devices
    scale = 1.0 / (2.0 * local_rows * devices)
    blocks = []
    for point in range(points):
        start = jnp.int32(0)
        count = lax.axis_size("grid") * share
        band_k = bands[point]
        hband_k = hbands[point]
        band_cols = jnp.concatenate(
            [
                lax.dynamic_slice_in_dim(band_k, start, count, 1),
                lax.dynamic_slice_in_dim(band_k, half, count, 1),
            ],
            1,
        )
        summed = jnp.einsum("gi,gj->ij", band_cols, hband_k, preferred_element_type=jnp.float32)
        hband_cols = jnp.concatenate(
            [
                lax.dynamic_slice_in_dim(hband_k, start, count, 1),
                lax.dynamic_slice_in_dim(hband_k, half, count, 1),
            ],
            1,
        )
        summed = summed + jnp.einsum(
            "gi,gj->ij", hband_cols, band_k, preferred_element_type=jnp.float32
        )
        real_rows = (summed[:count, :half] + summed[count:, half:]) * scale
        imag_rows = (summed[:count, half:] - summed[count:, :half]) * scale
        blocks.append(
            lax.psum_scatter(
                jnp.concatenate([real_rows, imag_rows], 1), "grid", scatter_dimension=0, tiled=True
            )
        )
    hamiltonian = jnp.stack(blocks, 1)
    hamiltonian = jnp.transpose(hamiltonian, (1, 0, 2))
    ham_real = hamiltonian[:, :, :half]
    ham_imag = hamiltonian[:, :, half:]
    row_index = lax.axis_index("grid") * share + lax.iota(jnp.int32, share)
    col_index = lax.iota(jnp.int32, half)
    identity = (row_index[:, None] == col_index[None, :]).astype(jnp.float32)[None]
    trace_part = jnp.sum(ham_real * identity, axis=(1, 2))
    trace = lax.psum(trace_part, "grid")
    level = (trace / half)[:, None, None]
    centred = ham_real - level * identity
    squares = jnp.sum(centred * centred, axis=(1, 2)) + jnp.sum(ham_imag * ham_imag, axis=(1, 2))
    total = lax.psum(squares, "grid")
    spread = jnp.sqrt(total / half + 1e-06)[:, None, None]
    filling = (occupied.astype(jnp.float32) / half)[:, None, None]
    dens_real = filling * identity - centred / (4.0 * spread)
    dens_imag = -ham_imag / (4.0 * spread)
    density = jnp.concatenate([dens_real, dens_imag], 2).astype(jnp.bfloat16)
    for repeat in range(MCW):
        gathered = lax.all_gather(density, "grid", axis=1, tiled=True)
        matrix = embedding(gathered)
        square = jnp.einsum("krc,kcd->krd", density, matrix, preferred_element_type=jnp.float32)
        cube = jnp.einsum(
            "krc,kcd->krd", square.astype(jnp.bfloat16), matrix, preferred_element_type=jnp.float32
        )
        density = (3.0 * square - 2.0 * cube).astype(jnp.bfloat16)
    gathered = lax.all_gather(density, "grid", axis=1, tiled=True)
    matrix = embedding(gathered)
    updated = jnp.einsum("kgc,kcd->kgd", bands, matrix, preferred_element_type=jnp.float32)
    return updated.astype(jnp.bfloat16)


def solution(mesh):
    return jax.shard_map(
        on_device,
        mesh=mesh,
        in_specs=(P("kset", "grid", None), P("kset", "grid", None), P("kset")),
        out_specs=P("kset", "grid", None),
        check_vma=False,
    )
```

profile of v0, /device:TPU:0, one launch (start us, length us, event | category | flops | bytes accessed | tf_op | source)
XLA Modules:
  0.0 426.6 jit_solution(12887339969295550722)
XLA Ops:
  6.5 3.0 fusion.32
  9.5 1.5 convolution_add_fusion.1
  11.0 0.6 fusion.23
  11.6 2.5 pad_maximum_fusion
  14.1 6.1 %copy.18 = f32[768,1536]{1,0:T(8,128)} copy(f32[768,1536]{0,1:T(8,128)} %pad_maximum_fusion) | data formatting | bytes 9437184
  20.1 0.0 reduce-scatter.7.cloned.1.call-update
  20.1 0.0 reduce-scatter.9.cloned.1.call-start
  20.2 1.4 fusion.27
  21.6 1.5 convolution_add_fusion
  23.1 0.6 fusion.21
  23.7 2.5 pad_maximum_fusion.1
  26.2 6.2 %copy.20 = f32[768,1536]{1,0:T(8,128)} copy(f32[768,1536]{0,1:T(8,128)} %pad_maximum_fusion.1) | data formatting | bytes 9437184
  32.4 0.0 reduce-scatter.9.cloned.1.call-update
  32.5 0.0 all-gather.4.cloned.1.call-start
  32.5 0.1 fusion.46
  32.6 65.9 %reduce-scatter.7.cloned.1.call-done = f32[48,1536]{1,0:T(8,128)} async-done(((f32[768,1536]{1,0:T(8,128)}), f32[48,1536]{1,0:T(8,128)}) %reduce-scatter.7.cloned.1.call-update) | async-done | bytes 294928
  98.5 1.2 copy.19
  99.7 0.2 copy.9
  100.0 77.6 %reduce-scatter.9.cloned.1.call-done = f32[48,1536]{1,0:T(8,128)} async-done(((f32[768,1536]{1,0:T(8,128)}), f32[48,1536]{1,0:T(8,128)}) %reduce-scatter.9.cloned.1.call-update) | async-done | bytes 294928
  177.6 1.2 copy.21
  178.8 0.2 copy.10
  179.1 0.1 multiply_reduce_fusion.2
  179.2 30.0 %psum.14 = f32[2]{0:T(128)S(1)} all-reduce(f32[2]{0:T(128)S(1)} %multiply_reduce_fusion.2), channel_id=1, replica_groups=mesh['kset'=2,'grid'=16] {'grid'}, use_global_device_ids=true, to_apply=%region_3.0 | all-reduce | flops 2 | bytes 16 | tf_op jit(solution)/shard_map/psum | solution.py:63
  209.2 0.2 multiply_reduce_fusion
  209.4 29.5 %psum.15 = f32[2]{0:T(128)S(1)} all-reduce(f32[2]{0:T(128)S(1)} %add.42), channel_id=1, replica_groups=mesh['kset'=2,'grid'=16] {'grid'}, use_global_device_ids=true, to_apply=%region_6.0 | all-reduce | flops 2 | bytes 16 | tf_op jit(solution)/shard_map/psum | solution.py:67
  238.9 0.2 subtract_convert_fusion
  239.1 1.0 copy.11
  240.1 0.0 all-gather.4.cloned.1.call-update
  240.2 0.2 all-gather.6.cloned.1.call-start
  240.4 50.4 %all-gather.4.cloned.1.call-done = bf16[2,768,1536]{2,0,1:T(2,128)(2,1)} async-done(((bf16[2,48,1536]{2,0,1:T(2,128)(2,1)}), bf16[2,768,1536]{2,0,1:T(2,128)(2,1)}) %all-gather.4.cloned.1.call-update) | async-done | bytes 4718608 | tf_op jit(solution)/shard_map/all_gather | solution.py:74
  290.8 3.1 copy.14
  293.9 0.3 slice_negate_fusion.2
  294.2 1.9 fusion.9
  296.0 2.5 fusion.25
  298.6 0.0 all-gather.6.cloned.1.call-update
  298.6 0.0 copy-start.4
  298.6 0.0 all-gather.8.cloned.1.call-start
  298.6 51.9 %all-gather.6.cloned.1.call-done = bf16[2,768,1536]{2,1,0:T(8,128)(2,1)} async-done(((bf16[2,48,1536]{2,1,0:T(8,128)(2,1)}), bf16[2,768,1536]{2,1,0:T(8,128)(2,1)}) %all-gather.6.cloned.1.call-update) | async-done | bytes 4718608 | tf_op jit(solution)/shard_map/all_gather | solution.py:74
  350.6 2.8 slice_negate_fusion.1
  353.4 0.9 copy-done.2
  354.3 1.9 fusion.7
  356.2 2.5 fusion.24
  358.7 0.0 all-gather.8.cloned.1.call-update
  358.7 52.0 %all-gather.8.cloned.1.call-done = bf16[2,768,1536]{2,1,0:T(8,128)(2,1)} async-done(((bf16[2,48,1536]{2,1,0:T(8,128)(2,1)}), bf16[2,768,1536]{2,1,0:T(8,128)(2,1)}) %all-gather.8.cloned.1.call-update) | async-done | bytes 4718608 | tf_op jit(solution)/shard_map/all_gather | solution.py:81
  410.7 2.8 slice_negate_fusion
  413.5 0.9 copy-done.3
  414.4 4.0 fusion.13
  418.4 1.6 copy.16
  (17 shorter events, 0.1 us)
Async XLA Ops:
  6.5 3.0 copy-start.1
  6.5 3.0 copy-start
  6.5 92.0 %reduce-scatter.7.cloned.1.call-start = ((), (), s32[]{:S(2)}) async-start(), calls=%async_computation.5 | async-start | bytes 5013504
  20.1 157.4 %reduce-scatter.9.cloned.1.call-start = ((), (), s32[]{:S(2)}) async-start(), calls=%async_computation.6 | async-start | bytes 5013504
  32.4 177.0 %copy-start.5 = (s32[2]{0:T(128)S(1)}, s32[2]{0:T(128)}, u32[]{:S(2)}) copy-start(s32[2]{0:T(128)} %param.5) | copy-start | bytes 28
  32.5 258.3 %all-gather.4.cloned.1.call-start = ((), (), s32[]{:S(2)}) async-start(), calls=%async_computation.2 | async-start | bytes 5013504 | tf_op jit(solution)/shard_map/all_gather | solution.py:74
  240.2 110.4 %all-gather.6.cloned.1.call-start = ((), (), s32[]{:S(2)}) async-start(), calls=%async_computation.3 | async-start | bytes 5013504 | tf_op jit(solution)/shard_map/all_gather | solution.py:74
  298.6 54.8 %copy-start.4 = (bf16[2,48,1536]{2,1,0:T(8,128)(2,1)S(1)}, bf16[2,48,1536]{2,1,0:T(8,128)(2,1)}, u32[]{:S(2)}) copy-start(bf16[2,48,1536]{2,1,0:T(8,128)(2,1)} %fusion.25) | copy-start | bytes 884740
  298.6 112.1 %all-gather.8.cloned.1.call-start = ((), (), s32[]{:S(2)}) async-start(), calls=%async_computation.4 | async-start | bytes 5013504 | tf_op jit(solution)/shard_map/all_gather | solution.py:81
  350.6 3.8 copy-start.2
  410.7 3.8 copy-start.3
Sparse Core Ops, SparseCore 0:
  20.3 78.2 reduce-scatter.6
  102.9 74.6 reduce-scatter.8
  240.3 50.4 all-gather.3
  298.7 51.8 all-gather.5
  358.9 51.7 all-gather.7
where the time goes:
time: 427 us
  waiting for transfers between devices  298 us (70%)
  blocking collectives  59.5 us (14%)
  local copies, waits for them, and re-layouts  22.7 us (5%)
  matrix products  20.1 us (5%)
  between operations  13.3 us (3%)
  other arithmetic  12.8 us (3%)
    all_gather x3, waiting for transfers between devices, on_device(): gathered = lax.all_gather(density, 'grid', axis=1, tiled=True)  154 us
    unnamed x7, waiting for transfers between devices  144 us
    psum x1, blocking collectives, on_device(): trace = lax.psum(trace_part, 'grid')  30 us
    psum x1, blocking collectives, on_device(): total = lax.psum(squares, 'grid')  29.5 us
    unnamed x16, local copies, waits for them, and re-layouts  16.5 us
  transfers between devices with their start and end apart: 5, of which 5 were waited for; matrix products, arithmetic and copies ran while one was open for 3% of the time, Pallas kernels for 0%

commit v1 on v0

--- a/solution.py
+++ b/solution.py
@@ -4,6 +4,19 @@
 from jax.sharding import PartitionSpec as P
 
 MCW = 2
+
+
+def ring_gather(shard, axis, dim):
+    ways = lax.axis_size(axis)
+    up = [(d, (d + 1) % ways) for d in range(ways)]
+    down = [(d, (d - 1) % ways) for d in range(ways)]
+    earlier, later = ([shard], [shard])
+    for _ in range(ways // 2):
+        earlier.append(lax.ppermute(earlier[-1], axis, up))
+    for _ in range((ways - 1) // 2):
+        later.append(lax.ppermute(later[-1], axis, down))
+    line = jnp.concatenate([*earlier[::-1], *later[1:]], axis=dim)
+    return jnp.roll(line, (lax.axis_index(axis) - ways // 2) * shard.shape[dim], axis=dim)
 
 
 def embedding(full):
@@ -71,7 +84,7 @@
     dens_imag = -ham_imag / (4.0 * spread)
     density = jnp.concatenate([dens_real, dens_imag], 2).astype(jnp.bfloat16)
     for repeat in range(MCW):
-        gathered = lax.all_gather(density, "grid", axis=1, tiled=True)
+        gathered = ring_gather(density, "grid", 1)
         matrix = embedding(gathered)
         square = jnp.einsum("krc,kcd->krd", density, matrix, preferred_element_type=jnp.float32)
         cube = jnp.einsum(

time: 427 us -> 480 us (1.12)
  starting transfers between devices: 0.35 us -> 63.5 us
  waiting for transfers between devices: 298 us -> 276 us
  other arithmetic: 12.8 us -> 20.4 us
    all_gather x3 -> x1, waiting for transfers between devices: 154 us -> 54.1 us  [on_device(): gathered = lax.all_gather(density, 'grid', axis=1, tiled=True)]
    ppermute x0 -> x30, waiting for transfers between devices: none -> 78.4 us  [the longest x16 75 us: ring_gather(): earlier.append(lax.ppermute(earlier[-1], axis, up))]
    ppermute x0 -> x30, starting transfers between devices: none -> 63.4 us  [the longest x14 63.2 us: ring_gather(): later.append(lax.ppermute(later[-1], axis, down))]
    concatenate x0 -> x2, other arithmetic: none -> 10 us  [ring_gather(): jnp.roll(line, (lax.axis_index(axis) - ways // 2) * shard.shape[dim], axi...]
    unnamed x16 -> x55, local copies, waits for them, and re-layouts: 16.5 us -> 24.4 us
    unnamed x7 -> x5, waiting for transfers between devices: 144 us -> 144 us
  transfers between devices with their start and end apart: 5 -> 33, of which waited for: 5 -> 22; matrix products, arithmetic and copies ran while one was open for 3% -> 4% of each run, Pallas kernels for 0% -> 0%
where the time goes in v1:
time: 480 us; the launch traced here: 479 us
  waiting for transfers between devices  276 us (58%)
  starting transfers between devices  63.5 us (13%)
  blocking collectives  59.5 us (12%)
  local copies, waits for them, and re-layouts  26.5 us (6%)
  other arithmetic  20.4 us (4%)
  matrix products  19.5 us (4%)
  between operations  13.6 us (3%)
    unnamed x5, waiting for transfers between devices  144 us
    ppermute x16, waiting for transfers between devices, ring_gather(): earlier.append(lax.ppermute(earlier[-1], axis, up))  75 us
    ppermute x14, starting transfers between devices, ring_gather(): later.append(lax.ppermute(later[-1], axis, down))  63.2 us
    all_gather x1, waiting for transfers between devices, on_device(): gathered = lax.all_gather(density, 'grid', axis=1, tiled=True)  54.1 us
    psum x1, blocking collectives, on_device(): trace = lax.psum(trace_part, 'grid')  30 us
    psum x1, blocking collectives, on_device(): total = lax.psum(squares, 'grid')  29.5 us
    unnamed x55, local copies, waits for them, and re-layouts  24.4 us
    concatenate x2, other arithmetic, ring_gather(): jnp.roll(line, (lax.axis_index(axis) - ways // 2) * shard.shape[dim], axi...  10 us
  transfers between devices with their start and end apart: 33, of which 22 were waited for; matrix products, arithmetic and copies ran while one was open for 4% of the time, Pallas kernels for 0%

profile of v1, /device:TPU:0, one launch (start us, length us, event | category | flops | bytes accessed | tf_op | source)
XLA Modules:
  0.0 479.0 jit_solution(8477917129008728734)
XLA Ops:
  6.5 3.0 fusion.30
  11.6 2.5 pad_maximum_fusion
  14.1 6.1 %copy.14 = f32[768,1536]{1,0:T(8,128)} copy(f32[768,1536]{0,1:T(8,128)} %pad_maximum_fusion) | data formatting | bytes 9437184
  23.7 2.5 pad_maximum_fusion.1
  26.3 6.2 %copy.16 = f32[768,1536]{1,0:T(8,128)} copy(f32[768,1536]{0,1:T(8,128)} %pad_maximum_fusion.1) | data formatting | bytes 9437184
  32.6 65.9 %reduce-scatter.7.cloned.1.call-done = f32[48,1536]{1,0:T(8,128)} async-done(((f32[768,1536]{1,0:T(8,128)}), f32[48,1536]{1,0:T(8,128)}) %reduce-scatter.7.cloned.1.call-update) | async-done | bytes 294928
  100.0 77.6 %reduce-scatter.9.cloned.1.call-done = f32[48,1536]{1,0:T(8,128)} async-done(((f32[768,1536]{1,0:T(8,128)}), f32[48,1536]{1,0:T(8,128)}) %reduce-scatter.9.cloned.1.call-update) | async-done | bytes 294928
  179.2 30.0 %psum.14 = f32[2]{0:T(128)S(1)} all-reduce(f32[2]{0:T(128)S(1)} %multiply_reduce_fusion.2), channel_id=1, replica_groups=mesh['kset'=2,'grid'=16] {'grid'}, use_global_device_ids=true, to_apply=%region_3.0 | all-reduce | flops 2 | bytes 16 | tf_op jit(solution)/shard_map/psum | solution.py:76
  209.5 29.5 %psum.15 = f32[2]{0:T(128)S(1)} all-reduce(f32[2]{0:T(128)S(1)} %add.51), channel_id=1, replica_groups=mesh['kset'=2,'grid'=16] {'grid'}, use_global_device_ids=true, to_apply=%region_6.0 | all-reduce | flops 2 | bytes 16 | tf_op jit(solution)/shard_map/psum | solution.py:80
  239.2 8.8 %collective-permute-done = bf16[2,48,1536]{2,1,0:T(8,128)(2,1)S(1)} collective-permute-done((bf16[2,48,1536]{2,1,0:T(8,128)(2,1)S(1)}, bf16[2,48,1536]{2,1,0:T(8,128)(2,1)S(1)}, u32[]{:S(2)}, u32[]{:S(2)}) %collective-permute-start) | collective-permute-done | bytes 294944 | tf_op jit(solution)/shard_map/ppermute | solution.py:15
  248.1 4.4 collective-permute-start.8
  252.5 4.4 collective-permute-done.1
  256.9 4.5 collective-permute-start.9
  261.4 4.4 collective-permute-done.2
  265.9 4.5 collective-permute-start.10
  270.4 4.4 collective-permute-done.3
  275.5 4.5 collective-permute-start.11
  280.1 3.7 collective-permute-done.4
  285.0 4.7 collective-permute-start.12
  289.7 3.0 collective-permute-done.5
  294.0 4.8 %collective-permute-start.13 = (bf16[2,48,1536]{2,1,0:T(8,128)(2,1)}, bf16[2,48,1536]{2,1,0:T(8,128)(2,1)}, u32[]{:S(2)}, u32[]{:S(2)}) collective-permute-start(bf16[2,48,1536]{2,1,0:T(8,128)(2,1)} %collective-permute-done.12), channel_id=1, source_target_pairs={{0,15},{1,0},{2,1},{3,2},{4,3},{5,4},{6,5},{7,6},{8,7},{9,8},{10,9... | collective-permute-start | bytes 884744 | tf_op jit(solution)/shard_map/ppermute | solution.py:17
  298.8 3.0 collective-permute-done.6
  303.3 4.6 collective-permute-start.14
  307.9 3.0 collective-permute-done.7
  318.1 5.0 %fusion.7 = bf16[2,768,1536]{2,1,0:T(8,128)(2,1)S(1)} fusion(s32[]{:T(128)S(6)} %select_n.13, bf16[2,768,1536]{2,1,0:T(8,128)(2,1)S(1)} %constant_dynamic-update-slice_fusion), kind=kLoop, calls=%fused_computation.15 | loop fusion | flops 9437184 | bytes 9437188 | tf_op jit(solution)/shard_map/jit(_roll_dynamic)/concatenate | solution.py:19
  323.5 1.9 fusion.11
  325.3 1.9 subtract_convert_fusion.1
  327.3 8.9 %collective-permute-done.15 = bf16[2,48,1536]{2,1,0:T(8,128)(2,1)S(1)} collective-permute-done((bf16[2,48,1536]{2,1,0:T(8,128)(2,1)S(1)}, bf16[2,48,1536]{2,1,0:T(8,128)(2,1)S(1)}, u32[]{:S(2)}, u32[]{:S(2)}) %collective-permute-start.15) | collective-permute-done | bytes 294944 | tf_op jit(solution)/shard_map/ppermute | solution.py:15
  336.2 4.4 collective-permute-start.23
  340.6 4.5 collective-permute-done.16
  345.2 4.4 collective-permute-start.24
  349.6 4.5 collective-permute-done.17
  354.1 4.4 collective-permute-start.25
  358.5 4.5 collective-permute-done.18
  363.1 4.4 collective-permute-start.26
  367.5 4.5 collective-permute-done.19
  372.0 4.4 collective-permute-start.27
  376.4 4.5 collective-permute-done.20
  381.0 4.4 collective-permute-start.28
  385.4 4.5 collective-permute-done.21
  389.9 4.4 collective-permute-start.29
  394.3 4.4 collective-permute-done.22
  399.2 5.0 %fusion.6 = bf16[2,768,1536]{2,1,0:T(8,128)(2,1)S(1)} fusion(s32[]{:T(128)S(6)} %select_n.13, bf16[2,768,1536]{2,1,0:T(8,128)(2,1)S(1)} %constant_dynamic-update-slice_fusion.16), kind=kLoop, calls=%fused_computation.14 | loop fusion | flops 9437184 | bytes 9437188 | tf_op jit(solution)/shard_map/jit(_roll_dynamic)/concatenate | solution.py:19
  404.6 1.9 fusion.9
  406.5 2.5 subtract_convert_fusion
  409.0 54.1 %all-gather.2.cloned.1.call-done = bf16[2,768,1536]{2,1,0:T(8,128)(2,1)} async-done(((bf16[2,48,1536]{2,1,0:T(8,128)(2,1)}), bf16[2,768,1536]{2,1,0:T(8,128)(2,1)}) %all-gather.2.cloned.1.call-update) | async-done | bytes 4718608 | tf_op jit(solution)/shard_map/all_gather | solution.py:94
  463.1 2.8 slice_negate_fusion
  466.9 4.0 fusion.15
  (113 shorter events, 24.8 us)
Async XLA Ops:
  6.5 3.0 copy-start.1
  6.5 3.0 copy-start
  6.5 92.0 %reduce-scatter.7.cloned.1.call-start = ((), (), s32[]{:S(2)}) async-start(), calls=%async_computation.3 | async-start | bytes 5013504
  20.2 157.4 %reduce-scatter.9.cloned.1.call-start = ((), (), s32[]{:S(2)}) async-start(), calls=%async_computation.4 | async-start | bytes 5013504
  32.5 177.0 %copy-start.10 = (s32[2]{0:T(128)S(1)}, s32[2]{0:T(128)}, u32[]{:S(2)}) copy-start(s32[2]{0:T(128)} %param.7) | copy-start | bytes 28
  32.5 430.6 %all-gather.2.cloned.1.call-start = ((), (), s32[]{:S(2)}) async-start(), calls=%async_computation.2 | async-start | bytes 5013504 | tf_op jit(solution)/shard_map/all_gather | solution.py:94
  239.2 8.9 %collective-permute-start = (bf16[2,48,1536]{2,1,0:T(8,128)(2,1)S(1)}, bf16[2,48,1536]{2,1,0:T(8,128)(2,1)S(1)}, u32[]{:S(2)}, u32[]{:S(2)}) collective-permute-start(bf16[2,48,1536]{2,1,0:T(8,128)(2,1)S(1)} %pad_maximum_fusion.2), channel_id=1, source_target_pairs={{0,1},{1,2},{2,3},{3,4},{4,5},{5,6},{6,7},{7,8},{8,9},{9,10},{10,1... | collective-permute-start | bytes 884744 | tf_op jit(solution)/shard_map/ppermute | solution.py:15
  248.0 8.8 %collective-permute-start.1 = (bf16[2,48,1536]{2,1,0:T(8,128)(2,1)S(1)}, bf16[2,48,1536]{2,1,0:T(8,128)(2,1)S(1)}, u32[]{:S(2)}, u32[]{:S(2)}) collective-permute-start(bf16[2,48,1536]{2,1,0:T(8,128)(2,1)S(1)} %collective-permute-done), channel_id=1, source_target_pairs={{0,1},{1,2},{2,3},{3,4},{4,5},{5,6},{6,7},{7,8},{8,9},{9,10},{10,1... | collective-permute-start | bytes 884744 | tf_op jit(solution)/shard_map/ppermute | solution.py:15
  248.1 8.8 %collective-permute-start.8 = (bf16[2,48,1536]{2,1,0:T(8,128)(2,1)S(1)}, bf16[2,48,1536]{2,1,0:T(8,128)(2,1)S(1)}, u32[]{:S(2)}, u32[]{:S(2)}) collective-permute-start(bf16[2,48,1536]{2,1,0:T(8,128)(2,1)S(1)} %pad_maximum_fusion.2), channel_id=1, source_target_pairs={{0,15},{1,0},{2,1},{3,2},{4,3},{5,4},{6,5},{7,6},{8,7},{9,8},{10,9... | collective-permute-start | bytes 884744 | tf_op jit(solution)/shard_map/ppermute | solution.py:17
  256.9 8.9 %collective-permute-start.2 = (bf16[2,48,1536]{2,1,0:T(8,128)(2,1)S(1)}, bf16[2,48,1536]{2,1,0:T(8,128)(2,1)S(1)}, u32[]{:S(2)}, u32[]{:S(2)}) collective-permute-start(bf16[2,48,1536]{2,1,0:T(8,128)(2,1)S(1)} %collective-permute-done.1), channel_id=1, source_target_pairs={{0,1},{1,2},{2,3},{3,4},{4,5},{5,6},{6,7},{7,8},{8,9},{9,10},{10,1... | collective-permute-start | bytes 884744 | tf_op jit(solution)/shard_map/ppermute | solution.py:15
  256.9 8.9 %collective-permute-start.9 = (bf16[2,48,1536]{2,1,0:T(8,128)(2,1)S(1)}, bf16[2,48,1536]{2,1,0:T(8,128)(2,1)S(1)}, u32[]{:S(2)}, u32[]{:S(2)}) collective-permute-start(bf16[2,48,1536]{2,1,0:T(8,128)(2,1)S(1)} %collective-permute-done.8), channel_id=1, source_target_pairs={{0,15},{1,0},{2,1},{3,2},{4,3},{5,4},{6,5},{7,6},{8,7},{9,8},{10,9... | collective-permute-start | bytes 884744 | tf_op jit(solution)/shard_map/ppermute | solution.py:17
  265.8 8.9 %collective-permute-start.3 = (bf16[2,48,1536]{2,1,0:T(8,128)(2,1)S(1)}, bf16[2,48,1536]{2,1,0:T(8,128)(2,1)S(1)}, u32[]{:S(2)}, u32[]{:S(2)}) collective-permute-start(bf16[2,48,1536]{2,1,0:T(8,128)(2,1)S(1)} %collective-permute-done.2), channel_id=1, source_target_pairs={{0,1},{1,2},{2,3},{3,4},{4,5},{5,6},{6,7},{7,8},{8,9},{9,10},{10,1... | collective-permute-start | bytes 884744 | tf_op jit(solution)/shard_map/ppermute | solution.py:15
  265.9 9.0 %collective-permute-start.10 = (bf16[2,48,1536]{2,1,0:T(8,128)(2,1)S(1)}, bf16[2,48,1536]{2,1,0:T(8,128)(2,1)S(1)}, u32[]{:S(2)}, u32[]{:S(2)}) collective-permute-start(bf16[2,48,1536]{2,1,0:T(8,128)(2,1)S(1)} %collective-permute-done.9), channel_id=1, source_target_pairs={{0,15},{1,0},{2,1},{3,2},{4,3},{5,4},{6,5},{7,6},{8,7},{9,8},{10,9... | collective-permute-start | bytes 884744 | tf_op jit(solution)/shard_map/ppermute | solution.py:17
  274.8 19.2 %copy-start.7 = (bf16[2,48,1536]{2,1,0:T(8,128)(2,1)}, bf16[2,48,1536]{2,1,0:T(8,128)(2,1)S(1)}, u32[]{:S(2)}) copy-start(bf16[2,48,1536]{2,1,0:T(8,128)(2,1)S(1)} %collective-permute-done.3) | copy-start | bytes 884740
  274.8 8.9 %collective-permute-start.4 = (bf16[2,48,1536]{2,1,0:T(8,128)(2,1)S(1)}, bf16[2,48,1536]{2,1,0:T(8,128)(2,1)S(1)}, u32[]{:S(2)}, u32[]{:S(2)}) collective-permute-start(bf16[2,48,1536]{2,1,0:T(8,128)(2,1)S(1)} %collective-permute-done.3), channel_id=1, source_target_pairs={{0,1},{1,2},{2,3},{3,4},{4,5},{5,6},{6,7},{7,8},{8,9},{9,10},{10,1... | collective-permute-start | bytes 884744 | tf_op jit(solution)/shard_map/ppermute | solution.py:15
  274.8 0.7 copy-start.3
  275.5 8.8 %collective-permute-start.11 = (bf16[2,48,1536]{2,1,0:T(8,128)(2,1)S(1)}, bf16[2,48,1536]{2,1,0:T(8,128)(2,1)S(1)}, u32[]{:S(2)}, u32[]{:S(2)}) collective-permute-start(bf16[2,48,1536]{2,1,0:T(8,128)(2,1)S(1)} %collective-permute-done.10), channel_id=1, source_target_pairs={{0,15},{1,0},{2,1},{3,2},{4,3},{5,4},{6,5},{7,6},{8,7},{9,8},{10,9... | collective-permute-start | bytes 884744 | tf_op jit(solution)/shard_map/ppermute | solution.py:17
  283.7 15.0 %copy-start.8 = (bf16[2,48,1536]{2,1,0:T(8,128)(2,1)}, bf16[2,48,1536]{2,1,0:T(8,128)(2,1)S(1)}, u32[]{:S(2)}) copy-start(bf16[2,48,1536]{2,1,0:T(8,128)(2,1)S(1)} %collective-permute-done.4) | copy-start | bytes 884740
  283.7 8.9 %collective-permute-start.5 = (bf16[2,48,1536]{2,1,0:T(8,128)(2,1)S(1)}, bf16[2,48,1536]{2,1,0:T(8,128)(2,1)S(1)}, u32[]{:S(2)}, u32[]{:S(2)}) collective-permute-start(bf16[2,48,1536]{2,1,0:T(8,128)(2,1)S(1)} %collective-permute-done.4), channel_id=1, source_target_pairs={{0,1},{1,2},{2,3},{3,4},{4,5},{5,6},{6,7},{7,8},{8,9},{9,10},{10,1... | collective-permute-start | bytes 884744 | tf_op jit(solution)/shard_map/ppermute | solution.py:15
  284.3 0.7 copy-start.5
  285.0 8.9 %collective-permute-start.12 = (bf16[2,48,1536]{2,1,0:T(8,128)(2,1)S(1)}, bf16[2,48,1536]{2,1,0:T(8,128)(2,1)}, u32[]{:S(2)}, u32[]{:S(2)}) collective-permute-start(bf16[2,48,1536]{2,1,0:T(8,128)(2,1)S(1)} %collective-permute-done.11), channel_id=1, source_target_pairs={{0,15},{1,0},{2,1},{3,2},{4,3},{5,4},{6,5},{7,6},{8,7},{9,8},{10,9... | collective-permute-start | bytes 884744 | tf_op jit(solution)/shard_map/ppermute | solution.py:17
  292.7 9.1 %copy-start.9 = (bf16[2,48,1536]{2,1,0:T(8,128)(2,1)}, bf16[2,48,1536]{2,1,0:T(8,128)(2,1)S(1)}, u32[]{:S(2)}) copy-start(bf16[2,48,1536]{2,1,0:T(8,128)(2,1)S(1)} %collective-permute-done.5) | copy-start | bytes 884740
  292.7 9.1 %collective-permute-start.6 = (bf16[2,48,1536]{2,1,0:T(8,128)(2,1)S(1)}, bf16[2,48,1536]{2,1,0:T(8,128)(2,1)}, u32[]{:S(2)}, u32[]{:S(2)}) collective-permute-start(bf16[2,48,1536]{2,1,0:T(8,128)(2,1)S(1)} %collective-permute-done.5), channel_id=1, source_target_pairs={{0,1},{1,2},{2,3},{3,4},{4,5},{5,6},{6,7},{7,8},{8,9},{9,10},{10,1... | collective-permute-start | bytes 884744 | tf_op jit(solution)/shard_map/ppermute | solution.py:15
  294.0 9.4 %collective-permute-start.13 = (bf16[2,48,1536]{2,1,0:T(8,128)(2,1)}, bf16[2,48,1536]{2,1,0:T(8,128)(2,1)}, u32[]{:S(2)}, u32[]{:S(2)}) collective-permute-start(bf16[2,48,1536]{2,1,0:T(8,128)(2,1)} %collective-permute-done.12), channel_id=1, source_target_pairs={{0,15},{1,0},{2,1},{3,2},{4,3},{5,4},{6,5},{7,6},{8,7},{9,8},{10,9... | collective-permute-start | bytes 884744 | tf_op jit(solution)/shard_map/ppermute | solution.py:17
  301.8 9.2 %collective-permute-start.7 = (bf16[2,48,1536]{2,1,0:T(8,128)(2,1)}, bf16[2,48,1536]{2,1,0:T(8,128)(2,1)}, u32[]{:S(2)}, u32[]{:S(2)}) collective-permute-start(bf16[2,48,1536]{2,1,0:T(8,128)(2,1)} %collective-permute-done.6), channel_id=1, source_target_pairs={{0,1},{1,2},{2,3},{3,4},{4,5},{5,6},{6,7},{7,8},{8,9},{9,10},{10,1... | collective-permute-start | bytes 884744 | tf_op jit(solution)/shard_map/ppermute | solution.py:15
  301.8 14.3 %copy-start.4 = (bf16[2,48,1536]{2,1,0:T(8,128)(2,1)S(1)}, bf16[2,48,1536]{2,1,0:T(8,128)(2,1)}, u32[]{:S(2)}) copy-start(bf16[2,48,1536]{2,1,0:T(8,128)(2,1)} %copy-done.3) | copy-start | bytes 884740
  301.8 14.3 %copy-start.6 = (bf16[2,48,1536]{2,1,0:T(8,128)(2,1)S(1)}, bf16[2,48,1536]{2,1,0:T(8,128)(2,1)}, u32[]{:S(2)}) copy-start(bf16[2,48,1536]{2,1,0:T(8,128)(2,1)} %copy-done.5) | copy-start | bytes 884740
  303.3 14.7 %collective-permute-start.14 = (bf16[2,48,1536]{2,1,0:T(8,128)(2,1)}, bf16[2,48,1536]{2,1,0:T(8,128)(2,1)S(1)}, u32[]{:S(2)}, u32[]{:S(2)}) collective-permute-start(bf16[2,48,1536]{2,1,0:T(8,128)(2,1)} %collective-permute-done.13), channel_id=1, source_target_pairs={{0,15},{1,0},{2,1},{3,2},{4,3},{5,4},{6,5},{7,6},{8,7},{9,8},{10,9... | collective-permute-start | bytes 884744 | tf_op jit(solution)/shard_map/ppermute | solution.py:17
  327.2 9.0 %collective-permute-start.15 = (bf16[2,48,1536]{2,1,0:T(8,128)(2,1)S(1)}, bf16[2,48,1536]{2,1,0:T(8,128)(2,1)S(1)}, u32[]{:S(2)}, u32[]{:S(2)}) collective-permute-start(bf16[2,48,1536]{2,1,0:T(8,128)(2,1)S(1)} %subtract_convert_fusion.1), channel_id=1, source_target_pairs={{0,1},{1,2},{2,3},{3,4},{4,5},{5,6},{6,7},{7,8},{8,9},{9,10},{10,1... | collective-permute-start | bytes 884744 | tf_op jit(solution)/shard_map/ppermute | solution.py:15
  336.2 8.9 %collective-permute-start.16 = (bf16[2,48,1536]{2,1,0:T(8,128)(2,1)S(1)}, bf16[2,48,1536]{2,1,0:T(8,128)(2,1)S(1)}, u32[]{:S(2)}, u32[]{:S(2)}) collective-permute-start(bf16[2,48,1536]{2,1,0:T(8,128)(2,1)S(1)} %collective-permute-done.15), channel_id=1, source_target_pairs={{0,1},{1,2},{2,3},{3,4},{4,5},{5,6},{6,7},{7,8},{8,9},{9,10},{10,1... | collective-permute-start | bytes 884744 | tf_op jit(solution)/shard_map/ppermute | solution.py:15
  336.2 9.0 %collective-permute-start.23 = (bf16[2,48,1536]{2,1,0:T(8,128)(2,1)S(1)}, bf16[2,48,1536]{2,1,0:T(8,128)(2,1)S(1)}, u32[]{:S(2)}, u32[]{:S(2)}) collective-permute-start(bf16[2,48,1536]{2,1,0:T(8,128)(2,1)S(1)} %subtract_convert_fusion.1), channel_id=1, source_target_pairs={{0,15},{1,0},{2,1},{3,2},{4,3},{5,4},{6,5},{7,6},{8,7},{9,8},{10,9... | collective-permute-start | bytes 884744 | tf_op jit(solution)/shard_map/ppermute | solution.py:17
  345.1 8.9 %collective-permute-start.17 = (bf16[2,48,1536]{2,1,0:T(8,128)(2,1)S(1)}, bf16[2,48,1536]{2,1,0:T(8,128)(2,1)S(1)}, u32[]{:S(2)}, u32[]{:S(2)}) collective-permute-start(bf16[2,48,1536]{2,1,0:T(8,128)(2,1)S(1)} %collective-permute-done.16), channel_id=1, source_target_pairs={{0,1},{1,2},{2,3},{3,4},{4,5},{5,6},{6,7},{7,8},{8,9},{9,10},{10,1... | collective-permute-start | bytes 884744 | tf_op jit(solution)/shard_map/ppermute | solution.py:15
  345.2 8.9 %collective-permute-start.24 = (bf16[2,48,1536]{2,1,0:T(8,128)(2,1)S(1)}, bf16[2,48,1536]{2,1,0:T(8,128)(2,1)S(1)}, u32[]{:S(2)}, u32[]{:S(2)}) collective-permute-start(bf16[2,48,1536]{2,1,0:T(8,128)(2,1)S(1)} %collective-permute-done.23), channel_id=1, source_target_pairs={{0,15},{1,0},{2,1},{3,2},{4,3},{5,4},{6,5},{7,6},{8,7},{9,8},{10,9... | collective-permute-start | bytes 884744 | tf_op jit(solution)/shard_map/ppermute | solution.py:17
  354.1 8.9 %collective-permute-start.18 = (bf16[2,48,1536]{2,1,0:T(8,128)(2,1)S(1)}, bf16[2,48,1536]{2,1,0:T(8,128)(2,1)S(1)}, u32[]{:S(2)}, u32[]{:S(2)}) collective-permute-start(bf16[2,48,1536]{2,1,0:T(8,128)(2,1)S(1)} %collective-permute-done.17), channel_id=1, source_target_pairs={{0,1},{1,2},{2,3},{3,4},{4,5},{5,6},{6,7},{7,8},{8,9},{9,10},{10,1... | collective-permute-start | bytes 884744 | tf_op jit(solution)/shard_map/ppermute | solution.py:15
  354.1 8.9 %collective-permute-start.25 = (bf16[2,48,1536]{2,1,0:T(8,128)(2,1)S(1)}, bf16[2,48,1536]{2,1,0:T(8,128)(2,1)S(1)}, u32[]{:S(2)}, u32[]{:S(2)}) collective-permute-start(bf16[2,48,1536]{2,1,0:T(8,128)(2,1)S(1)} %collective-permute-done.24), channel_id=1, source_target_pairs={{0,15},{1,0},{2,1},{3,2},{4,3},{5,4},{6,5},{7,6},{8,7},{9,8},{10,9... | collective-permute-start | bytes 884744 | tf_op jit(solution)/shard_map/ppermute | solution.py:17
  363.0 8.9 %collective-permute-start.19 = (bf16[2,48,1536]{2,1,0:T(8,128)(2,1)S(1)}, bf16[2,48,1536]{2,1,0:T(8,128)(2,1)S(1)}, u32[]{:S(2)}, u32[]{:S(2)}) collective-permute-start(bf16[2,48,1536]{2,1,0:T(8,128)(2,1)S(1)} %collective-permute-done.18), channel_id=1, source_target_pairs={{0,1},{1,2},{2,3},{3,4},{4,5},{5,6},{6,7},{7,8},{8,9},{9,10},{10,1... | collective-permute-start | bytes 884744 | tf_op jit(solution)/shard_map/ppermute | solution.py:15
  363.1 8.9 %collective-permute-start.26 = (bf16[2,48,1536]{2,1,0:T(8,128)(2,1)S(1)}, bf16[2,48,1536]{2,1,0:T(8,128)(2,1)S(1)}, u32[]{:S(2)}, u32[]{:S(2)}) collective-permute-start(bf16[2,48,1536]{2,1,0:T(8,128)(2,1)S(1)} %collective-permute-done.25), channel_id=1, source_target_pairs={{0,15},{1,0},{2,1},{3,2},{4,3},{5,4},{6,5},{7,6},{8,7},{9,8},{10,9... | collective-permute-start | bytes 884744 | tf_op jit(solution)/shard_map/ppermute | solution.py:17
  372.0 8.9 %collective-permute-start.20 = (bf16[2,48,1536]{2,1,0:T(8,128)(2,1)S(1)}, bf16[2,48,1536]{2,1,0:T(8,128)(2,1)S(1)}, u32[]{:S(2)}, u32[]{:S(2)}) collective-permute-start(bf16[2,48,1536]{2,1,0:T(8,128)(2,1)S(1)} %collective-permute-done.19), channel_id=1, source_target_pairs={{0,1},{1,2},{2,3},{3,4},{4,5},{5,6},{6,7},{7,8},{8,9},{9,10},{10,1... | collective-permute-start | bytes 884744 | tf_op jit(solution)/shard_map/ppermute | solution.py:15
  372.0 8.9 %collective-permute-start.27 = (bf16[2,48,1536]{2,1,0:T(8,128)(2,1)S(1)}, bf16[2,48,1536]{2,1,0:T(8,128)(2,1)S(1)}, u32[]{:S(2)}, u32[]{:S(2)}) collective-permute-start(bf16[2,48,1536]{2,1,0:T(8,128)(2,1)S(1)} %collective-permute-done.26), channel_id=1, source_target_pairs={{0,15},{1,0},{2,1},{3,2},{4,3},{5,4},{6,5},{7,6},{8,7},{9,8},{10,9... | collective-permute-start | bytes 884744 | tf_op jit(solution)/shard_map/ppermute | solution.py:17
  380.9 8.9 %collective-permute-start.21 = (bf16[2,48,1536]{2,1,0:T(8,128)(2,1)S(1)}, bf16[2,48,1536]{2,1,0:T(8,128)(2,1)S(1)}, u32[]{:S(2)}, u32[]{:S(2)}) collective-permute-start(bf16[2,48,1536]{2,1,0:T(8,128)(2,1)S(1)} %collective-permute-done.20), channel_id=1, source_target_pairs={{0,1},{1,2},{2,3},{3,4},{4,5},{5,6},{6,7},{7,8},{8,9},{9,10},{10,1... | collective-permute-start | bytes 884744 | tf_op jit(solution)/shard_map/ppermute | solution.py:15
  381.0 8.9 %collective-permute-start.28 = (bf16[2,48,1536]{2,1,0:T(8,128)(2,1)S(1)}, bf16[2,48,1536]{2,1,0:T(8,128)(2,1)S(1)}, u32[]{:S(2)}, u32[]{:S(2)}) collective-permute-start(bf16[2,48,1536]{2,1,0:T(8,128)(2,1)S(1)} %collective-permute-done.27), channel_id=1, source_target_pairs={{0,15},{1,0},{2,1},{3,2},{4,3},{5,4},{6,5},{7,6},{8,7},{9,8},{10,9... | collective-permute-start | bytes 884744 | tf_op jit(solution)/shard_map/ppermute | solution.py:17
  389.9 8.8 %collective-permute-start.22 = (bf16[2,48,1536]{2,1,0:T(8,128)(2,1)S(1)}, bf16[2,48,1536]{2,1,0:T(8,128)(2,1)S(1)}, u32[]{:S(2)}, u32[]{:S(2)}) collective-permute-start(bf16[2,48,1536]{2,1,0:T(8,128)(2,1)S(1)} %collective-permute-done.21), channel_id=1, source_target_pairs={{0,1},{1,2},{2,3},{3,4},{4,5},{5,6},{6,7},{7,8},{8,9},{9,10},{10,1... | collective-permute-start | bytes 884744 | tf_op jit(solution)/shard_map/ppermute | solution.py:15
  389.9 9.3 %collective-permute-start.29 = (bf16[2,48,1536]{2,1,0:T(8,128)(2,1)S(1)}, bf16[2,48,1536]{2,1,0:T(8,128)(2,1)S(1)}, u32[]{:S(2)}, u32[]{:S(2)}) collective-permute-start(bf16[2,48,1536]{2,1,0:T(8,128)(2,1)S(1)} %collective-permute-done.28), channel_id=1, source_target_pairs={{0,15},{1,0},{2,1},{3,2},{4,3},{5,4},{6,5},{7,6},{8,7},{9,8},{10,9... | collective-permute-start | bytes 884744 | tf_op jit(solution)/shard_map/ppermute | solution.py:17
  463.1 3.8 copy-start.2
Sparse Core Ops, SparseCore 0:
  20.3 78.2 reduce-scatter.6
  102.9 74.6 reduce-scatter.8
  409.1 53.9 all-gather.1
